TPU v7x, 32 devices: a whole 2x2x4 slice. The times are simulated.
32 devices in a mesh: tok: 8 (over z, x), col: 4 (over y, core).
Axes of the slice: x: 2, y: 2, z: 4, core: 2. Of those that a mesh axis runs over, the one named last changes fastest.
Arguments:
- tokens: bfloat16 [2560, 4096], P('tok', 'col'), may hold values from -16 to 16
- w_query: bfloat16 [4096, 2048], P(None, 'col'), may hold values from -0.09375 to 0.09375
- w_key: bfloat16 [4096, 512], P(None, 'col'), may hold values from -0.09375 to 0.09375
- w_value: bfloat16 [4096, 512], P(None, 'col'), may hold values from -0.09375 to 0.09375
- w_out: bfloat16 [2048, 4096], P('col'), may hold values from -0.125 to 0.125
- block_ids: int32 [16, 40, 16], P('col', 'tok'), may hold values from 0 to 39, as said below
- block_counts: int32 [16, 40], P('col', 'tok'), may hold values from 1 to 16, as said below
Outputs:
- mixed: bfloat16 [2560, 4096], P('tok', 'col')
Inputs may be any that keep to these rules, and one draw needn't show every extreme that they name: block_ids[h, b, 0] = b; the slots below block_counts[h, b] hold distinct blocks none after b; later slots hold block numbers that are not read. block_counts[h, b] <= b + 1; densities differ from head to head, and some row of some head uses all 16 slots.
All inputs are finite; a program needn't handle non-finite values.
Results may differ from a plain program's by a relative error of at most 0.012.
Values may be sent and summed in bfloat16 or wider, within the bound.
No kernel may reach another device: no remote copies, remote signals or barrier semaphores. Data moves between devices by JAX's collectives and lax.ppermute only.
A program may use at most 64 MiB of HBM per device.

v0:
```python
import jax
import jax.numpy as jnp
from jax import lax
from jax.sharding import PartitionSpec as P

HEAD_SIZE = 128
BLK = 64
NSEL = 16
rope_base = 500000.0


def rotate(field, positions):
    half = field.shape[-1] // 2
    freq = rope_base ** (-jnp.arange(half, dtype=jnp.float32) / half)
    angle = positions[:, None] * freq[None, :]
    cosine = jnp.cos(angle)[:, None, :]
    sine = jnp.sin(angle)[:, None, :]
    first = field[..., :half]
    second = field[..., half:]
    return jnp.concatenate(
        [first * cosine - second * sine, second * cosine + first * sine], axis=-1
    )


def on_device(tokens, w_query, w_key, w_value, w_out, block_ids, block_counts):
    tok_rows = tokens.shape[0]
    head_local = w_query.shape[1] // HEAD_SIZE
    kv_local = w_key.shape[1] // HEAD_SIZE
    group_size = head_local // kv_local
    blocks_dev = block_ids.shape[1]
    piece = lax.all_gather(tokens, "col", axis=1, tiled=True)
    width = piece.shape[1]

    def product(weight):
        return jnp.dot(piece, weight, preferred_element_type=jnp.float32)

    query_raw = product(w_query)
    key_raw = product(w_key)
    value_raw = product(w_value)
    tok_place = lax.axis_index("tok")
    query_index = tok_place * tok_rows + jnp.arange(tok_rows, dtype=jnp.int32)
    positions = query_index.astype(jnp.float32)
    query_rows = rotate(query_raw.reshape(tok_rows, head_local, HEAD_SIZE), positions).astype(
        jnp.bfloat16
    )
    keys = rotate(key_raw.reshape(tok_rows, kv_local, HEAD_SIZE), positions).astype(jnp.bfloat16)
    values = value_raw.astype(jnp.bfloat16).reshape(tok_rows, kv_local, HEAD_SIZE)
    grouped = query_rows.reshape(tok_rows, kv_local, group_size, HEAD_SIZE)
    live = jnp.arange(NSEL, dtype=jnp.int32)[None, None, :] < block_counts[:, :, None]
    last_query = tok_place * tok_rows + tok_rows - 1
    start_state = (
        jnp.full((head_local, tok_rows), -1e30, jnp.float32),
        jnp.zeros((head_local, tok_rows), jnp.float32),
        jnp.zeros((head_local, tok_rows, HEAD_SIZE), jnp.float32),
    )
    key_part = lax.all_gather(keys, "tok", axis=0, tiled=True)
    value_part = lax.all_gather(values, "tok", axis=0, tiled=True)
    amount = key_part.shape[0]
    width = 512
    key_blocks = key_part.reshape(amount // width, width, kv_local, HEAD_SIZE)
    value_blocks = value_part.reshape(amount // width, width, kv_local, HEAD_SIZE)
    offsets = jnp.arange(amount // width, dtype=jnp.int32) * width

    def one_block(state, inputs):
        key_block, value_block, offset = inputs

        def compute(inner_state):
            highest, total, summed_weights = inner_state
            key_index = offset + jnp.arange(width, dtype=jnp.int32)
            key_group = key_index // BLK
            hit = jnp.any(
                (block_ids[:, :, :, None] == key_group[None, None, None, :]) & live[..., None],
                axis=2,
            )
            allowed = jnp.broadcast_to(hit[:, :, None, :], (head_local, blocks_dev, BLK, width))
            allowed = allowed.reshape(head_local, tok_rows, width)
            allowed = allowed & (key_index[None, None, :] <= query_index[None, :, None])
            logit_scores = jnp.einsum(
                "tcgd,kcd->cgtk", grouped, key_block, preferred_element_type=jnp.float32
            )
            logit_scores = logit_scores.reshape(head_local, tok_rows, width) * HEAD_SIZE ** (-0.5)
            masked = jnp.where(allowed, logit_scores, -1e30)
            fresh = jnp.maximum(highest, jnp.max(masked, axis=-1))
            decay = jnp.exp(highest - fresh)
            weights = jnp.where(allowed, jnp.exp(masked - fresh[..., None]), 0.0)
            total = total * decay + jnp.sum(weights, axis=-1)
            rounded_scores = weights.astype(jnp.bfloat16).reshape(
                kv_local, group_size, tok_rows, width
            )
            added = jnp.einsum(
                "cgtk,kcd->cgtd", rounded_scores, value_block, preferred_element_type=jnp.float32
            )
            summed_weights = summed_weights * decay[..., None] + added.reshape(
                head_local, tok_rows, HEAD_SIZE
            )
            return (fresh, total, summed_weights)

        return (
            lax.cond(offset > last_query, lambda inner_state: inner_state, compute, state),
            None,
        )

    result, _ = lax.scan(one_block, start_state, (key_blocks, value_blocks, offsets))
    highest, total, summed_weights = result
    attended = jnp.transpose((summed_weights / total[..., None]).astype(jnp.bfloat16), (1, 0, 2))
    flat = attended.reshape(tok_rows, head_local * HEAD_SIZE)
    summed_out = lax.psum_scatter(
        lax.dot_general(
            w_out, flat, (((0,), (1,)), ((), ())), preferred_element_type=jnp.float32
        ).astype(jnp.bfloat16),
        "col",
        scatter_dimension=0,
        tiled=True,
    ).astype(jnp.float32)
    return jnp.transpose(summed_out).astype(jnp.bfloat16)


def solution(mesh):
    in_specs = (
        P("tok", "col"),
        P(None, "col"),
        P(None, "col"),
        P(None, "col"),
        P("col", None),
        P("col", "tok", None),
        P("col", "tok"),
    )
    out_specs = P("tok", "col")
    return jax.shard_map(
        on_device, mesh=mesh, in_specs=in_specs, out_specs=out_specs, check_vma=False
    )
```

profile of v0, /device:TPU:0, one launch (start us, length us, event | category | flops | bytes accessed | tf_op | source)
XLA Modules:
  0.0 185.4 jit_solution(4791514653528160586)
XLA Ops:
  6.5 0.0 copy-start
  6.5 0.0 all-gather.3.cloned.1.call-start
  6.5 0.7 all-gather.3.cloned.1.call-update
  7.3 0.0 reduce-scatter.2.cloned.1.call-start
  7.3 0.7 copy.25
  8.0 0.6 multiply_cosine_fusion
  8.7 28.5 %all-gather.3.cloned.1.call-done = bf16[320,4096]{1,0:T(8,128)(2,1)} async-done(((bf16[320,1024]{1,0:T(8,128)(2,1)}), bf16[320,4096]{1,0:T(8,128)(2,1)}) %all-gather.3.cloned.1.call-update) | async-done | bytes 2621456 | tf_op jit(solution)/shard_map/all_gather | solution.py:31
  37.2 4.5 %fusion.43 = f32[320,512]{1,0:T(8,128)S(1)} fusion(bf16[320,4096]{1,0:T(8,128)(2,1)} %all-gather.3.cloned.1.call-done, bf16[4096,512]{1,0:T(8,128)(2,1)} %param.12), kind=kOutput, calls=%fused_computation.67 | convolution fusion | flops 1342177280 | bytes 7471104 | tf_op jit(solution)/shard_map/dot_general | solution.py:35
  41.7 0.2 reshape.338
  41.9 0.0 copy-start.1
  41.9 0.4 fusion.42
  42.3 0.0 copy-done
  42.3 1.3 copy-done.1
  43.7 0.0 copy-start.2
  43.7 0.8 convolution_bitcast_fusion
  44.5 0.7 fusion.39
  45.2 0.1 pad_maximum_fusion.1
  45.3 31.9 %all_gather.10 = bf16[2560,1,128]{2,0,1:T(8,128)(2,1)S(1)} all-gather(bf16[320,1,128]{2,0,1:T(8,128)(2,1)S(1)} %pad_maximum_fusion.1), channel_id=1, replica_groups=mesh['tok'=8,'col'=4] {'tok'}, dimensions={0}, use_global_device_ids=true | all-gather | bytes 737280 | tf_op jit(solution)/shard_map/all_gather | solution.py:56
  77.3 0.0 copy-done.2
  77.3 0.8 convolution_convert_fusion.1
  78.1 0.0 copy-start.3
  78.2 31.4 %all-gather = bf16[2560,128]{1,0:T(8,128)(2,1)S(1)} all-gather(bf16[320,128]{1,0:T(8,128)(2,1)S(1)} %convolution_convert_fusion.1), channel_id=2, replica_groups=mesh['tok'=8,'col'=4] {'tok'}, dimensions={0}, use_global_device_ids=true | all-gather | bytes 737280 | tf_op jit(solution)/shard_map/all_gather | solution.py:57
  109.6 0.2 fusion.29
  109.7 0.2 pad_maximum_fusion
  110.0 0.0 copy-done.3
  110.0 11.1 %while.15 = (s32[]{:T(128)}, f32[4,320]{1,0:T(4,128)S(1)}, f32[4,320]{1,0:T(4,128)S(1)}, f32[4,320,128]{2,1,0:T(8,128)S(1)}, s32[5]{0:T(128)S(1)}, /*index=5*/s3...) while((s32[]{:T(128)}, f32[4,320]{1,0:T(4,128)S(1)}, ...), condition=%wide.region_6.7_spmd.clone, body=%wide.region_0.6_spmd.clone.sunk | while | flops 347014272 | bytes 13164303 | solution.py:103
  110.0 0.6 dynamic_slice.33
  111.3 4.4 %conditional.3 = (f32[4,320]{1,0:T(4,128)S(1)}, f32[4,320]{1,0:T(4,128)S(1)}, f32[4,320,128]{2,1,0:T(8,128)S(1)}) conditional(s32[]{:T(128)} %convert_element_type.74, (s32[4,5,16]{2,1,0:T(8,128)S(1)}, s32[]{:T(128)}, s32[4,5,16]{2,1,0:T(8,128)S(1)}, s32[]{:T(128)}, bf16[5,512,1,128]{3,1,2,0:T(8,128)(2,1)S(1)}, /*index=5*/s32[]{:T(128)}, ...), branch_computations={%region_1.4_spmd, %region_5.5_spmd} | conditional | flops 347014272 | bytes 13151224 | solution.py:99
  111.3 0.6 add_select_fusion
  112.0 0.1 broadcast_compare_fusion.1
  112.0 0.3 and_reduce_fusion
  112.3 0.2 broadcast_in_dim.4
  112.5 0.2 broadcast_compare_fusion
  112.7 0.8 fusion.4
  113.5 1.1 fusion.6
  114.6 1.0 fusion.11
  115.7 0.6 dynamic_slice.33
  117.0 0.6 dynamic_slice.33
  118.4 0.6 dynamic_slice.33
  119.7 0.6 dynamic_slice.33
  121.1 5.3 %fusion.28 = bf16[4096,320]{0,1:T(8,128)(2,1)} fusion(bf16[512,4096]{1,0:T(8,128)(2,1)} %param.15, f32[4,320,128]{2,1,0:T(8,128)S(1)} %get-tuple-element.165, f32[4,320]{1,0:T(4,128)S(1)} %get-tuple-element.166), kind=kOutput, calls=%fused_computation.38 | convolution fusion | flops 1343815680 | bytes 7476224 | tf_op jit(solution)/shard_map/dot_general | solution.py:108
  126.4 0.0 reduce-scatter.2.cloned.1.call-update
  126.4 52.1 %reduce-scatter.2.cloned.1.call-done = bf16[1024,320]{0,1:T(8,128)(2,1)} async-done(((bf16[4096,320]{0,1:T(8,128)(2,1)}), bf16[1024,320]{0,1:T(8,128)(2,1)}) %reduce-scatter.2.cloned.1.call-update) | async-done | bytes 655376 | tf_op jit(solution)/shard_map/reduce_scatter | solution.py:107
  (32 shorter events, 0.3 us)
Async XLA Ops:
  6.5 35.8 %copy-start = (bf16[4096,128]{1,0:T(8,128)(2,1)S(1)}, bf16[4096,128]{1,0:T(8,128)(2,1)}, u32[]{:S(2)}) copy-start(bf16[4096,128]{1,0:T(8,128)(2,1)} %param.13) | copy-start | bytes 3145732
  6.5 30.6 %all-gather.3.cloned.1.call-start = ((), (), s32[]{:S(2)}) async-start(), calls=%async_computation.1 | async-start | bytes 3276800 | tf_op jit(solution)/shard_map/all_gather | solution.py:31
  7.3 171.3 %reduce-scatter.2.cloned.1.call-start = ((), (), s32[]{:S(2)}) async-start(), calls=%async_computation.2 | async-start | bytes 3276800 | tf_op jit(solution)/shard_map/reduce_scatter | solution.py:107
  41.9 1.7 copy-start.1
  43.7 33.6 %copy-start.2 = (bf16[4096,128]{1,0:T(8,128)(2,1)S(1)}, bf16[4096,128]{1,0:T(8,128)(2,1)}, u32[]{:S(2)}) copy-start(bf16[4096,128]{1,0:T(8,128)(2,1)} %param.14) | copy-start | bytes 3145732
  78.1 31.9 %copy-start.3 = (s32[4,5]{1,0:T(4,128)S(1)}, s32[4,5]{1,0:T(4,128)}, u32[]{:S(2)}) copy-start(s32[4,5]{1,0:T(4,128)} %param.17) | copy-start | bytes 244
Sparse Core Ops, SparseCore 0:
  8.9 28.2 all-gather.2
  126.5 51.9 reduce-scatter.1
where the time goes:
time: 186 us; the launch traced here: 185 us
  waiting for transfers between devices  81.4 us (44%)
  blocking collectives  63.3 us (34%)
  between operations  13.5 us (7%)
  matrix products  13.4 us (7%)
  local copies, waits for them, and re-layouts  6.13 us (3%)
  other arithmetic  4.08 us (2%)
  loops' own time  3.5 us (2%)
    reduce_scatter x1, waiting for transfers between devices, on_device(): lax.psum_scatter(lax.dot_general(w_out, flat, (((0,), (1,)), ((), ())), p...  52.1 us
    all_gather x1, blocking collectives, on_device(): key_part = lax.all_gather(keys, 'tok', axis=0, tiled=True)  31.9 us
    all_gather x1, blocking collectives, on_device(): value_part = lax.all_gather(values, 'tok', axis=0, tiled=True)  31.4 us
    all_gather x1, waiting for transfers between devices, on_device(): piece = lax.all_gather(tokens, 'col', axis=1, tiled=True)  28.5 us
    dot_general x3, matrix products, product(): return jnp.dot(piece, weight, preferred_element_type=jnp.float32)  6.19 us
    dot_general x1, matrix products, on_device(): lax.dot_general(w_out, flat, (((0,), (1,)), ((), ())), preferred_element_...  5.31 us
  transfers between devices with their start and end apart: 2, of which 2 were waited for; matrix products, arithmetic and copies ran while one was open for 1% of the time, Pallas kernels for 0%

commit v1 on v0

--- a/solution.py
+++ b/solution.py
@@ -7,6 +7,19 @@
 BLK = 64
 NSEL = 16
 rope_base = 500000.0
+
+
+def collect(shard, axis, dim):
+    size, index, width = (lax.axis_size(axis), lax.axis_index(axis), shard.shape[dim])
+    right = [(i, (i + 1) % size) for i in range(size)]
+    out = jnp.zeros((*shard.shape[:dim], size * width, *shard.shape[dim + 1 :]), shard.dtype)
+    current = shard
+    for step in range(size):
+        holder = (index - step) % size
+        out = lax.dynamic_update_slice_in_dim(out, current, holder * width, axis=dim)
+        if step < size - 1:
+            current = lax.ppermute(current, axis, right)
+    return out
 
 
 def rotate(field, positions):
@@ -53,7 +66,7 @@
         jnp.zeros((head_local, tok_rows), jnp.float32),
         jnp.zeros((head_local, tok_rows, HEAD_SIZE), jnp.float32),
     )
-    key_part = lax.all_gather(keys, "tok", axis=0, tiled=True)
+    key_part = collect(keys, "tok", 0)
     value_part = lax.all_gather(values, "tok", axis=0, tiled=True)
     amount = key_part.shape[0]
     width = 512

time: 186 us -> 197 us (1.059)
  waiting for transfers between devices: 81.4 us -> 117 us
  blocking collectives: 63.3 us -> 31.8 us
  starting transfers between devices: 0.04 us -> 2.1 us
  local copies, waits for them, and re-layouts: 6.13 us -> 8.16 us
    ppermute x0 -> x7, waiting for transfers between devices: none -> 41.5 us  [collect(): current = lax.ppermute(current, axis, right)]
    all_gather x1 -> x0, blocking collectives: 31.9 us -> none  [on_device(): key_part = lax.all_gather(keys, 'tok', axis=0, tiled=True)]
    reduce_scatter x1, waiting for transfers between devices: 52.1 us -> 47.6 us  [on_device(): lax.psum_scatter(lax.dot_general(w_out, flat, (((0,), (1,)), ((), ())), p...]
    ppermute x0 -> x7, starting transfers between devices: none -> 2.06 us  [collect(): current = lax.ppermute(current, axis, right)]
    dot_general x3, matrix products: 6.19 us -> 8.16 us  [product(): return jnp.dot(piece, weight, preferred_element_type=jnp.float32)]
  transfers between devices with their start and end apart: 2 -> 9, of which waited for: 2 -> 8; matrix products, arithmetic and copies ran while one was open for 1% -> 5% of each run, Pallas kernels for 0% -> 0%
where the time goes in v1:
time: 197 us
  waiting for transfers between devices  117 us (59%)
  blocking collectives  31.8 us (16%)
  matrix products  15.3 us (8%)
  between operations  13.7 us (7%)
  local copies, waits for them, and re-layouts  8.16 us (4%)
  other arithmetic  4.87 us (2%)
  loops' own time  3.61 us (2%)
  starting transfers between devices  2.1 us (1%)
    reduce_scatter x1, waiting for transfers between devices, on_device(): lax.psum_scatter(lax.dot_general(w_out, flat, (((0,), (1,)), ((), ())), p...  47.6 us
    ppermute x7, waiting for transfers between devices, collect(): current = lax.ppermute(current, axis, right)  41.5 us
    all_gather x1, blocking collectives, on_device(): value_part = lax.all_gather(values, 'tok', axis=0, tiled=True)  31.8 us
    all_gather x1, waiting for transfers between devices, on_device(): piece = lax.all_gather(tokens, 'col', axis=1, tiled=True)  27.6 us
    dot_general x3, matrix products, product(): return jnp.dot(piece, weight, preferred_element_type=jnp.float32)  8.16 us
    dot_general x1, matrix products, on_device(): lax.dot_general(w_out, flat, (((0,), (1,)), ((), ())), preferred_element_...  5.27 us
  transfers between devices with their start and end apart: 9, of which 8 were waited for; matrix products, arithmetic and copies ran while one was open for 5% of the time, Pallas kernels for 0%

profile of v1, /device:TPU:0, one launch (start us, length us, event | category | flops | bytes accessed | tf_op | source)
XLA Modules:
  0.0 197.0 jit_solution(11368420216935468100)
XLA Ops:
  6.5 0.7 all-gather.3.cloned.1.call-update
  7.3 0.0 reduce-scatter.2.cloned.1.call-start
  7.5 0.7 copy.23
  8.2 1.4 multiply_cosine_fusion
  9.6 27.6 %all-gather.3.cloned.1.call-done = bf16[320,4096]{1,0:T(8,128)(2,1)} async-done(((bf16[320,1024]{1,0:T(8,128)(2,1)}), bf16[320,4096]{1,0:T(8,128)(2,1)}) %all-gather.3.cloned.1.call-update) | async-done | bytes 2621456 | tf_op jit(solution)/shard_map/all_gather | solution.py:44
  37.2 2.7 %convolution_bitcast_fusion = f32[320,1,128]{2,0,1:T(8,128)S(1)} fusion(bf16[320,4096]{1,0:T(8,128)(2,1)} %all-gather.3.cloned.1.call-done, bf16[4096,128]{1,0:T(8,128)(2,1)S(1)} %copy-done), kind=kOutput, calls=%fused_computation.39 | convolution fusion | flops 335544320 | bytes 3833856 | tf_op jit(solution)/shard_map/dot_general | solution.py:48
  39.9 0.7 fusion.39
  40.6 0.1 broadcast_in_dim.23
  40.7 0.1 constant_dynamic-update-slice_fusion.7
  40.9 1.5 collective-permute-start
  42.4 4.6 %fusion.43 = f32[320,512]{1,0:T(8,128)} fusion(bf16[320,4096]{1,0:T(8,128)(2,1)S(1)} %copy-done.1, bf16[4096,512]{1,0:T(8,128)(2,1)} %param.12), kind=kOutput, calls=%fused_computation.75 | convolution fusion | flops 1342177280 | bytes 7471104 | tf_op jit(solution)/shard_map/dot_general | solution.py:48
  47.0 1.4 reshape.338
  48.4 0.4 fusion.42
  48.8 1.3 copy-done.2
  50.1 0.8 convolution_convert_fusion.1
  51.0 31.8 %all-gather = bf16[2560,128]{1,0:T(8,128)(2,1)S(1)} all-gather(bf16[320,128]{1,0:T(8,128)(2,1)S(1)} %convolution_convert_fusion.1), channel_id=2, replica_groups=mesh['tok'=8,'col'=4] {'tok'}, dimensions={0}, use_global_device_ids=true | all-gather | bytes 737280 | tf_op jit(solution)/shard_map/all_gather | solution.py:70
  82.8 0.2 fusion.29
  83.0 0.2 pad_maximum_fusion
  83.2 0.5 collective-permute-start.1
  83.7 0.9 constant_dynamic-update-slice_fusion.6
  84.6 5.9 %collective-permute-done.1 = bf16[320,1,128]{2,0,1:T(8,128)(2,1)S(1)} collective-permute-done((bf16[320,1,128]{2,0,1:T(8,128)(2,1)}, bf16[320,1,128]{2,0,1:T(8,128)(2,1)S(1)}, u32[]{:S(2)}, u32[]{:S(2)}) %collective-permute-start.1) | collective-permute-done | bytes 81952 | tf_op jit(solution)/shard_map/ppermute | solution.py:21
  90.6 7.1 %collective-permute-done.2 = bf16[320,1,128]{2,0,1:T(8,128)(2,1)S(1)} collective-permute-done((bf16[320,1,128]{2,0,1:T(8,128)(2,1)S(1)}, bf16[320,1,128]{2,0,1:T(8,128)(2,1)S(1)}, u32[]{:S(2)}, u32[]{:S(2)}) %collective-permute-start.2) | collective-permute-done | bytes 81952 | tf_op jit(solution)/shard_map/ppermute | solution.py:21
  97.7 0.0 collective-permute-start.3
  97.7 7.1 %collective-permute-done.3 = bf16[320,1,128]{2,0,1:T(8,128)(2,1)S(1)} collective-permute-done((bf16[320,1,128]{2,0,1:T(8,128)(2,1)S(1)}, bf16[320,1,128]{2,0,1:T(8,128)(2,1)S(1)}, u32[]{:S(2)}, u32[]{:S(2)}) %collective-permute-start.3) | collective-permute-done | bytes 81952 | tf_op jit(solution)/shard_map/ppermute | solution.py:21
  104.8 0.0 collective-permute-start.4
  104.9 7.1 %collective-permute-done.4 = bf16[320,1,128]{2,0,1:T(8,128)(2,1)S(1)} collective-permute-done((bf16[320,1,128]{2,0,1:T(8,128)(2,1)S(1)}, bf16[320,1,128]{2,0,1:T(8,128)(2,1)S(1)}, u32[]{:S(2)}, u32[]{:S(2)}) %collective-permute-start.4) | collective-permute-done | bytes 81952 | tf_op jit(solution)/shard_map/ppermute | solution.py:21
  112.0 0.0 collective-permute-start.5
  112.0 7.1 %collective-permute-done.5 = bf16[320,1,128]{2,0,1:T(8,128)(2,1)S(1)} collective-permute-done((bf16[320,1,128]{2,0,1:T(8,128)(2,1)S(1)}, bf16[320,1,128]{2,0,1:T(8,128)(2,1)S(1)}, u32[]{:S(2)}, u32[]{:S(2)}) %collective-permute-start.5) | collective-permute-done | bytes 81952 | tf_op jit(solution)/shard_map/ppermute | solution.py:21
  119.1 0.0 collective-permute-start.6
  119.1 7.1 %collective-permute-done.6 = bf16[320,1,128]{2,0,1:T(8,128)(2,1)S(1)} collective-permute-done((bf16[320,1,128]{2,0,1:T(8,128)(2,1)S(1)}, bf16[320,1,128]{2,0,1:T(8,128)(2,1)S(1)}, u32[]{:S(2)}, u32[]{:S(2)}) %collective-permute-start.6) | collective-permute-done | bytes 81952 | tf_op jit(solution)/shard_map/ppermute | solution.py:21
  126.4 10.9 %while.15 = (s32[]{:T(128)}, f32[4,320]{1,0:T(4,128)S(1)}, f32[4,320]{1,0:T(4,128)S(1)}, f32[4,320,128]{2,1,0:T(8,128)S(1)}, s32[5]{0:T(128)S(1)}, /*index=5*/s3...) while((s32[]{:T(128)}, f32[4,320]{1,0:T(4,128)S(1)}, ...), condition=%wide.region_6.7_spmd.clone, body=%wide.region_0.6_spmd.clone.sunk | while | flops 347014272 | bytes 13164303 | solution.py:116
  126.4 0.6 dynamic_slice.33
  127.6 4.4 %conditional.3 = (f32[4,320]{1,0:T(4,128)S(1)}, f32[4,320]{1,0:T(4,128)S(1)}, f32[4,320,128]{2,1,0:T(8,128)S(1)}) conditional(s32[]{:T(128)} %convert_element_type.74, (s32[4,5,16]{2,1,0:T(8,128)S(1)}, s32[]{:T(128)}, s32[4,5,16]{2,1,0:T(8,128)S(1)}, s32[]{:T(128)}, bf16[5,512,1,128]{3,1,2,0:T(8,128)(2,1)S(1)}, /*index=5*/s32[]{:T(128)}, ...), branch_computations={%region_1.4_spmd, %region_5.5_spmd} | conditional | flops 347014272 | bytes 13151224 | solution.py:112
  127.6 0.7 add_select_fusion
  128.3 0.1 broadcast_compare_fusion.1
  128.4 0.3 and_reduce_fusion
  128.6 0.2 broadcast_in_dim.4
  128.8 0.2 broadcast_compare_fusion
  129.0 0.8 fusion.4
  129.8 1.1 fusion.6
  131.0 1.0 fusion.11
  132.0 0.6 dynamic_slice.33
  133.4 0.6 dynamic_slice.33
  134.7 0.6 dynamic_slice.33
  136.0 0.6 dynamic_slice.33
  137.3 5.3 %fusion.28 = bf16[4096,320]{0,1:T(8,128)(2,1)} fusion(bf16[512,4096]{1,0:T(8,128)(2,1)} %param.15, f32[4,320,128]{2,1,0:T(8,128)S(1)} %get-tuple-element.165, f32[4,320]{1,0:T(4,128)S(1)} %get-tuple-element.166), kind=kOutput, calls=%fused_computation.38 | convolution fusion | flops 1343815680 | bytes 7476224 | tf_op jit(solution)/shard_map/dot_general | solution.py:121
  142.6 0.0 reduce-scatter.2.cloned.1.call-update
  142.6 47.6 %reduce-scatter.2.cloned.1.call-done = bf16[1024,320]{0,1:T(8,128)(2,1)} async-done(((bf16[4096,320]{0,1:T(8,128)(2,1)}), bf16[1024,320]{0,1:T(8,128)(2,1)}) %reduce-scatter.2.cloned.1.call-update) | async-done | bytes 655376 | tf_op jit(solution)/shard_map/reduce_scatter | solution.py:120
  (54 shorter events, 0.4 us)
Async XLA Ops:
  6.5 30.7 %copy-start = (bf16[4096,128]{1,0:T(8,128)(2,1)S(1)}, bf16[4096,128]{1,0:T(8,128)(2,1)}, u32[]{:S(2)}) copy-start(bf16[4096,128]{1,0:T(8,128)(2,1)} %param.13) | copy-start | bytes 3145732
  6.5 30.6 %all-gather.3.cloned.1.call-start = ((), (), s32[]{:S(2)}) async-start(), calls=%async_computation.1 | async-start | bytes 3276800 | tf_op jit(solution)/shard_map/all_gather | solution.py:44
  7.3 182.9 %reduce-scatter.2.cloned.1.call-start = ((), (), s32[]{:S(2)}) async-start(), calls=%async_computation.2 | async-start | bytes 3276800 | tf_op jit(solution)/shard_map/reduce_scatter | solution.py:120
  37.2 5.2 %copy-start.1 = (bf16[320,4096]{1,0:T(8,128)(2,1)S(1)}, bf16[320,4096]{1,0:T(8,128)(2,1)}, u32[]{:S(2)}) copy-start(bf16[320,4096]{1,0:T(8,128)(2,1)} %all-gather.3.cloned.1.call-done) | copy-start | bytes 7864324
  40.9 42.3 %collective-permute-start = (bf16[320,1,128]{2,0,1:T(8,128)(2,1)S(1)}, bf16[320,1,128]{2,0,1:T(8,128)(2,1)}, u32[]{:S(2)}, u32[]{:S(2)}) collective-permute-start(bf16[320,1,128]{2,0,1:T(8,128)(2,1)S(1)} %get-tuple-element.268), channel_id=1, source_target_pairs={{0,4},{4,8},{8,12},{12,16},{16,20},{20,24},{24,28},{28,0},{1,5},{5... | collective-permute-start | bytes 245768 | tf_op jit(solution)/shard_map/ppermute | solution.py:21
  47.0 1.8 copy-start.3
  48.4 1.7 copy-start.2
  50.1 32.7 %copy-start.4 = (f32[320,64]{1,0:T(8,128)S(1)}, f32[320,64]{1,0:T(8,128)}, u32[]{:S(2)}) copy-start(f32[320,64]{1,0:T(8,128)} %get-tuple-element.279) | copy-start | bytes 245764
  50.1 32.7 %copy-start.5 = (f32[320,64]{1,0:T(8,128)S(1)}, f32[320,64]{1,0:T(8,128)}, u32[]{:S(2)}) copy-start(f32[320,64]{1,0:T(8,128)} %get-tuple-element.280) | copy-start | bytes 245764
  82.8 43.6 %copy-start.6 = (s32[4,5]{1,0:T(4,128)S(1)}, s32[4,5]{1,0:T(4,128)}, u32[]{:S(2)}) copy-start(s32[4,5]{1,0:T(4,128)} %param.17) | copy-start | bytes 244
  83.2 7.4 %collective-permute-start.1 = (bf16[320,1,128]{2,0,1:T(8,128)(2,1)}, bf16[320,1,128]{2,0,1:T(8,128)(2,1)S(1)}, u32[]{:S(2)}, u32[]{:S(2)}) collective-permute-start(bf16[320,1,128]{2,0,1:T(8,128)(2,1)} %collective-permute-done), channel_id=1, source_target_pairs={{0,4},{4,8},{8,12},{12,16},{16,20},{20,24},{24,28},{28,0},{1,5},{5... | collective-permute-start | bytes 245768 | tf_op jit(solution)/shard_map/ppermute | solution.py:21
  90.6 7.1 %collective-permute-start.2 = (bf16[320,1,128]{2,0,1:T(8,128)(2,1)S(1)}, bf16[320,1,128]{2,0,1:T(8,128)(2,1)S(1)}, u32[]{:S(2)}, u32[]{:S(2)}) collective-permute-start(bf16[320,1,128]{2,0,1:T(8,128)(2,1)S(1)} %collective-permute-done.1), channel_id=1, source_target_pairs={{0,4},{4,8},{8,12},{12,16},{16,20},{20,24},{24,28},{28,0},{1,5},{5... | collective-permute-start | bytes 245768 | tf_op jit(solution)/shard_map/ppermute | solution.py:21
  97.7 7.1 %collective-permute-start.3 = (bf16[320,1,128]{2,0,1:T(8,128)(2,1)S(1)}, bf16[320,1,128]{2,0,1:T(8,128)(2,1)S(1)}, u32[]{:S(2)}, u32[]{:S(2)}) collective-permute-start(bf16[320,1,128]{2,0,1:T(8,128)(2,1)S(1)} %collective-permute-done.2), channel_id=1, source_target_pairs={{0,4},{4,8},{8,12},{12,16},{16,20},{20,24},{24,28},{28,0},{1,5},{5... | collective-permute-start | bytes 245768 | tf_op jit(solution)/shard_map/ppermute | solution.py:21
  104.8 7.1 %collective-permute-start.4 = (bf16[320,1,128]{2,0,1:T(8,128)(2,1)S(1)}, bf16[320,1,128]{2,0,1:T(8,128)(2,1)S(1)}, u32[]{:S(2)}, u32[]{:S(2)}) collective-permute-start(bf16[320,1,128]{2,0,1:T(8,128)(2,1)S(1)} %collective-permute-done.3), channel_id=1, source_target_pairs={{0,4},{4,8},{8,12},{12,16},{16,20},{20,24},{24,28},{28,0},{1,5},{5... | collective-permute-start | bytes 245768 | tf_op jit(solution)/shard_map/ppermute | solution.py:21
  112.0 7.1 %collective-permute-start.5 = (bf16[320,1,128]{2,0,1:T(8,128)(2,1)S(1)}, bf16[320,1,128]{2,0,1:T(8,128)(2,1)S(1)}, u32[]{:S(2)}, u32[]{:S(2)}) collective-permute-start(bf16[320,1,128]{2,0,1:T(8,128)(2,1)S(1)} %collective-permute-done.4), channel_id=1, source_target_pairs={{0,4},{4,8},{8,12},{12,16},{16,20},{20,24},{24,28},{28,0},{1,5},{5... | collective-permute-start | bytes 245768 | tf_op jit(solution)/shard_map/ppermute | solution.py:21
  119.1 7.1 %collective-permute-start.6 = (bf16[320,1,128]{2,0,1:T(8,128)(2,1)S(1)}, bf16[320,1,128]{2,0,1:T(8,128)(2,1)S(1)}, u32[]{:S(2)}, u32[]{:S(2)}) collective-permute-start(bf16[320,1,128]{2,0,1:T(8,128)(2,1)S(1)} %collective-permute-done.5), channel_id=1, source_target_pairs={{0,4},{4,8},{8,12},{12,16},{16,20},{20,24},{24,28},{28,0},{1,5},{5... | collective-permute-start | bytes 245768 | tf_op jit(solution)/shard_map/ppermute | solution.py:21
Sparse Core Ops, SparseCore 0:
  8.9 28.2 all-gather.2
  142.7 47.3 reduce-scatter.1
